TPU v7x, 32 devices: a whole 2x2x4 slice. The times are simulated.
32 devices in a mesh: mem: 4 (over y, x), gx: 4 (over z), gy: 2 (over core).
Axes of the slice: x: 2, y: 2, z: 4, core: 2. Of those that a mesh axis runs over, the one named last changes fastest.
Arguments:
- control: float32 [2, 16, 512, 512], P(None, 'mem', 'gx', 'gy'), may hold values from -6 to 6
- members: float32 [8, 2, 16, 256, 256], P('mem', None, None, 'gx', 'gy'), may hold values from -6 to 6
- diffusivity: float32 [16, 256, 256], P(None, 'gx', 'gy'), may hold values from 0.05 to 0.4
- rotation: float32 [256, 256], P('gx', 'gy'), may hold values from -1 to 1
Outputs:
- control_final: float32 [2, 16, 512, 512], P(None, 'mem', 'gx', 'gy')
- members_final: float32 [8, 2, 16, 256, 256], P('mem', None, None, 'gx', 'gy')
All inputs are finite; a program needn't handle non-finite values.
Results may differ from a plain program's by a relative error of at most 0.00002.
Values sent between devices are 32-bit elements; how exact they have to be, the bound alone decides.
A program may use at most 128 MiB of HBM per device.

v0:
```python
import functools

import jax
import jax.numpy as jnp
from jax import lax
from jax.experimental import pallas as pl
from jax.experimental.pallas import tpu as pltpu
from jax.sharding import PartitionSpec as P

CSTEPS = 4
MSTEPS = 4
H = 4
SLOT = 2 * H
LANES = 128

step_control = 0.15
viscosity = 0.5
step_member = 0.5
F32 = jnp.float32


def lane_ids(rows):
    return lax.broadcasted_iota(jnp.int32, (rows, LANES), 1)


def put_slot(packed, edges, slot):
    shift = H + SLOT * slot
    if not isinstance(slot, int):
        shift = lax.rem(shift, LANES)
    rolled = pltpu.roll(edges, shift, 1)
    ids = lane_ids(edges.shape[0])
    inside = (ids >= SLOT * slot) & (ids < SLOT * slot + SLOT)
    return jnp.where(inside, rolled, packed)


def side_block(left, right, slot):
    shift = lax.rem(2 * LANES - SLOT * slot - H, LANES)
    after = pltpu.roll(right, shift, 1)
    if left is right:
        return after
    before = pltpu.roll(left, shift, 1)
    return jnp.where(lane_ids(after.shape[0]) < LANES // 2, after, before)


def fused_kernel(
    copies, c_ref, m_ref, d_ref, r_ref, cf_ref, mf_ref,
    hc, tc, nc, prc, hm, tm, nm, prm, yc, ym, yc_in, ym_in, ccor, mcor, ccor_in, mcor_in,
    sums, sums_in, corr, hcorr, tcorr, ncorr, prcorr, ycorr, ycorr_in, kcor, kcor_in,
    shift, shift_in, send_sem, recv_sem,
):
    fields, clevels, crows, ccols = c_ref.shape
    count, _, levels, rows, cols = m_ref.shape
    base = count * fields
    nx, ny, n = lax.axis_size("gx"), lax.axis_size("gy"), lax.axis_size("mem")
    x, y, me = lax.axis_index("gx"), lax.axis_index("gy"), lax.axis_index("mem")
    two = ny > 2
    nsides = 2 if two else 1
    x_next, x_prev = {"gx": lax.rem(x + 1, nx)}, {"gx": lax.rem(x + nx - 1, nx)}
    y_next, y_prev = {"gy": lax.rem(y + 1, ny)}, {"gy": lax.rem(y + ny - 1, ny)}
    peers = [{"mem": lax.rem(me + k, n)} for k in range(1, n)]
    mesh_id = pl.DeviceIdType.MESH
    pending = []

    def send(src, dst, target):
        k = len(pending)
        copy = pltpu.make_async_remote_copy(
            src_ref=src, dst_ref=dst, send_sem=send_sem.at[k], recv_sem=recv_sem.at[k],
            device_id=target, device_id_type=mesh_id,
        )
        copy.start()
        pending.append(copy)
        return copy

    def landed(group):
        for copy in group:
            copy.wait_recv()

    def send_y(src, dst):
        group = [send(src, dst.at[0], y_next)]
        if two:
            group.append(send(src, dst.at[1], y_prev))
        return group

    def send_x(first, last, from_next, from_prev):
        return [send(first, from_next, x_prev), send(last, from_prev, x_next)]

    def send_corners(got, buf, buf_in):
        group = []
        for side in range(nsides):
            for g in range(got.shape[1]):
                tile = got[side, g]
                buf[side, 0, g] = tile[:H]
                buf[side, 1, g] = tile[tile.shape[0] - H :]
            group += send_x(
                buf.at[side, 0], buf.at[side, 1], buf_in.at[side, 0], buf_in.at[side, 1]
            )
        return group

    barrier = pltpu.get_barrier_semaphore()
    greeted = [x_next, x_prev, y_next] + ([y_prev] if two else []) + peers
    for target in greeted:
        pl.semaphore_signal(barrier, inc=1, device_id=target, device_id_type=mesh_id)

    ids = lane_ids(crows)
    yc[...] = jnp.zeros_like(yc)
    ym[...] = jnp.zeros_like(ym)
    ycorr[...] = jnp.zeros_like(ycorr)

    @pl.loop(0, clevels)
    def _(l):
        for f in range(fields):
            first = c_ref[f, l, :, :LANES]
            last = c_ref[f, l, :, ccols - LANES :]
            t = f * clevels + l
            yc[0] = put_slot(yc[0], jnp.where(ids < LANES // 2, first, last), t)
            hc[t] = c_ref[f, l, :H]
            tc[t] = c_ref[f, l, crows - H :]

    pl.semaphore_wait(barrier, len(greeted))
    got_yc = send_y(yc, yc_in)
    got_xc = send_x(hc, tc, nc, prc)

    @pl.loop(0, levels)
    def _(l):
        for f in range(fields):
            total = None
            for m in range(count):
                tile = m_ref[m, f, l]
                total = tile if total is None else total + tile
                g = m * fields + f
                ym[g] = put_slot(ym[g], tile, l)
                hm[g * levels + l] = tile[:H]
                tm[g * levels + l] = tile[rows - H :]
            sums[l, f] = total
        tile = d_ref[l]
        ym[base] = put_slot(ym[base], tile, l)
        hm[base * levels + l] = tile[:H]
        tm[base * levels + l] = tile[rows - H :]

    tile = r_ref[...]
    ym[base + 1] = put_slot(jnp.zeros((rows, LANES), F32), tile, 0)
    hm[(base + 1) * levels] = tile[:H]
    tm[(base + 1) * levels] = tile[rows - H :]
    got_ym = send_y(ym, ym_in)
    got_xm = send_x(hm, tm, nm, prm)
    got_sum = []
    for k in range(1, n):
        owner = lax.rem(me + k, n)
        got_sum.append(send(sums.at[pl.ds(owner * clevels, clevels)], sums_in.at[k - 1], peers[k - 1]))

    landed(got_yc)
    got_cc = send_corners(yc_in, ccor, ccor_in)
    landed(got_xc)
    landed(got_cc)

    def side_values(body, corners, g):
        out = [
            jnp.concatenate([body[s, g], corners[s, 0, g], corners[s, 1, g]], axis=0)
            for s in range(nsides)
        ]
        return out[0], out[-1]

    half_x, half_y = crows // 2, ccols // 2
    height, full = crows + 2 * H, ccols + LANES

    def control_level(l):
        left, right = side_values(yc_in, ccor_in, 0)
        body = []
        for f in range(fields):
            t = f * clevels + l
            own = jnp.concatenate([c_ref[f, l], nc[t], prc[t]], axis=0)
            body.append(jnp.concatenate([own, side_block(left, right, t)], axis=1))
        for _ in range(CSTEPS):
            a = body[0] * (0.5 * step_control)
            b = body[1] * (0.5 * step_control)
            new = []
            for f in body:
                ux = pltpu.roll(f, height - 1, 0)
                lx = pltpu.roll(f, 1, 0)
                uy = pltpu.roll(f, full - 1, 1)
                ly = pltpu.roll(f, 1, 1)
                lap = (ux + lx) + (uy + ly) - 4.0 * f
                new.append(f + ((step_control * viscosity) * lap - a * (ux - lx) - b * (uy - ly)))
            body = new
        pick_y = (
            lax.broadcasted_iota(jnp.int32, (ccols, half_y), 0) // 2
            == lax.broadcasted_iota(jnp.int32, (ccols, half_y), 1)
        ).astype(F32)
        pick_x = (
            lax.broadcasted_iota(jnp.int32, (half_x, crows), 1) // 2
            == lax.broadcasted_iota(jnp.int32, (half_x, crows), 0)
        ).astype(F32)
        for f in range(fields):
            field = body[f][:crows, :ccols]
            cf_ref[f, l] = field
            t = jnp.dot(field, pick_y, precision=lax.Precision.HIGHEST, preferred_element_type=F32)
            t = jnp.dot(pick_x, t, precision=lax.Precision.HIGHEST, preferred_element_type=F32)
            corr[l, f] = 0.25 * t

    landed(got_ym)
    got_mc = send_corners(ym_in, mcor, mcor_in)
    pl.loop(0, clevels)(control_level)
    landed(got_sum)

    @pl.loop(0, clevels)
    def _(l):
        for f in range(fields):
            total = sums[me * clevels + l, f]
            for k in range(n - 1):
                total = total + sums_in[k, l, f]
            tile = corr[l, f] - total * (1.0 / (count * n))
            corr[l, f] = tile
            ycorr[f] = put_slot(ycorr[f], tile, l)
            hcorr[f * clevels + l] = tile[:H]
            tcorr[f * clevels + l] = tile[rows - H :]

    got_yk = send_y(ycorr, ycorr_in)
    got_xk = send_x(hcorr, tcorr, ncorr, prcorr)
    landed(got_xm)
    landed(got_mc)

    mheight, mfull = rows + 2 * H, cols + LANES
    up_x = lambda f: pltpu.roll(f, mheight - 1, 0)
    low_x = lambda f: pltpu.roll(f, 1, 0)
    up_y = lambda f: pltpu.roll(f, mfull - 1, 1)
    low_y = lambda f: pltpu.roll(f, 1, 1)

    def extend(own, after, before, sides, slot):
        own = jnp.concatenate([own, after, before], axis=0)
        return jnp.concatenate([own, side_block(*sides, slot)], axis=1)

    def weights(l):
        t = base * levels + l
        kappa = extend(d_ref[l], nm[t], prm[t], side_values(ym_in, mcor_in, base), l)
        t = (base + 1) * levels
        spin = extend(r_ref[...], nm[t], prm[t], side_values(ym_in, mcor_in, base + 1), 0)
        east = (0.5 * step_member) * (kappa + up_x(kappa))
        north = (0.5 * step_member) * (kappa + up_y(kappa))
        return east, north, step_member * spin

    def steps(p, q, east, north, spin):
        for _ in range(MSTEPS):
            moved = []
            for f in (p, q):
                fx = east * (up_x(f) - f)
                fy = north * (up_y(f) - f)
                moved.append(f + ((fx - low_x(fx)) + (fy - low_y(fy))))
            p, q = moved[0] - spin * q, moved[1] + spin * p
        return p[:rows, :cols], q[:rows, :cols]

    def member_level(l):
        w = weights(l)
        for m in range(count):
            pair = []
            for f in range(fields):
                g = m * fields + f
                t = g * levels + l
                pair.append(extend(m_ref[m, f, l], nm[t], prm[t], side_values(ym_in, mcor_in, g), l))
            mf_ref[m, 0, l], mf_ref[m, 1, l] = steps(*pair, *w)

    def correction_level(l):
        w = weights(me * clevels + l)
        pair = []
        for f in range(fields):
            t = f * clevels + l
            pair.append(extend(corr[l, f], ncorr[t], prcorr[t], side_values(ycorr_in, kcor_in, f), l))
        shift[l, 0], shift[l, 1] = steps(*pair, *w)

    cut_a, cut_b = (3 * levels) // 16, (6 * levels) // 16
    pl.loop(0, cut_a)(member_level)
    landed(got_yk)
    got_kc = send_corners(ycorr_in, kcor, kcor_in)
    pl.loop(cut_a, cut_b)(member_level)
    landed(got_xk)
    landed(got_kc)
    pl.loop(0, clevels)(correction_level)
    got_shift = [send(shift, shift_in.at[k], peers[k]) for k in range(n - 1)]
    pl.loop(cut_b, levels)(member_level)

    def add(piece, owner):
        @pl.loop(0, clevels)
        def _(l):
            for f in range(fields):
                tile = piece[l, f]
                for m in range(count):
                    at = owner * clevels + l
                    mf_ref[m, f, at] = mf_ref[m, f, at] + tile

    add(shift, me)
    for k in range(n - 1):
        landed([got_shift[k]])
        add(shift_in.at[k], lax.rem(me + n - 1 - k, n))
    for copy in pending:
        copy.wait_send()
    assert len(pending) == copies


def per_device(control, members, diffusivity, rotation):
    fields, clevels, crows, ccols = control.shape
    count, _, levels, rows, cols = members.shape
    base = count * fields
    tiles = (base + 1) * levels + 1
    n = lax.axis_size("mem")
    ns = 2 if lax.axis_size("gy") > 2 else 1
    copies = 3 * (ns + 2 + 2 * ns) + 2 * (n - 1)
    vmem = lambda *shape: pltpu.VMEM(shape, F32)
    scratch = (
        [vmem(fields * clevels, H, ccols)] * 4
        + [vmem(tiles, H, cols)] * 4
        + [vmem(1, crows, LANES), vmem(base + 2, rows, LANES)]
        + [vmem(ns, 1, crows, LANES), vmem(ns, base + 2, rows, LANES)]
        + [vmem(ns, 2, 1, H, LANES), vmem(ns, 2, base + 2, H, LANES)] * 2
        + [vmem(levels, fields, rows, cols), vmem(n - 1, clevels, fields, rows, cols)]
        + [vmem(clevels, fields, rows, cols)]
        + [vmem(fields * clevels, H, cols)] * 4
        + [vmem(fields, rows, LANES), vmem(ns, fields, rows, LANES)]
        + [vmem(ns, 2, fields, H, LANES)] * 2
        + [vmem(clevels, fields, rows, cols), vmem(n - 1, clevels, fields, rows, cols)]
        + [pltpu.SemaphoreType.DMA((copies,))] * 2
    )
    return pl.pallas_call(
        functools.partial(fused_kernel, copies),
        in_specs=[pl.BlockSpec(memory_space=pltpu.VMEM)] * 4,
        out_specs=[pl.BlockSpec(memory_space=pltpu.VMEM)] * 2,
        out_shape=[
            jax.ShapeDtypeStruct(control.shape, F32),
            jax.ShapeDtypeStruct(members.shape, F32),
        ],
        scratch_shapes=scratch,
        compiler_params=pltpu.CompilerParams(collective_id=0, has_side_effects=True),
        name="fused",
    )(control, members, diffusivity, rotation)


def solution(mesh):
    in_specs = (
        P(None, "mem", "gx", "gy"),
        P("mem", None, None, "gx", "gy"),
        P(None, "gx", "gy"),
        P("gx", "gy"),
    )
    out_specs = (P(None, "mem", "gx", "gy"), P("mem", None, None, "gx", "gy"))
    return jax.shard_map(
        per_device, mesh=mesh, in_specs=in_specs, out_specs=out_specs, check_vma=False
    )
```

profile of v0, /device:TPU:0, one launch (start us, length us, event | category | flops | bytes accessed | tf_op | source)
XLA Modules:
  0.0 55.8 jit_solution(1954865608527600145)
XLA Ops:
  0.6 51.5 %fused.1 = (f32[2,4,128,256]{3,2,1,0:T(8,128)}, f32[2,2,16,64,128]{4,3,2,1,0:T(8,128)}) custom-call(f32[2,4,128,256]{3,2,1,0:T(8,128)} %c_ref.1, f32[2,2,16,64,128]{4,3,2,1,0:T(8,128)} %m_ref.1, f32[16,64,128]{2,1,0:T(8,128)} %d_ref.1, f32[64,128]{1,0:T(8,128)} %r_ref.1), custom_call_target="tpu_custom_call" | custom-call | tf_op jit(solution)/shard_map/fused/pallas_call | solution.py:321
  52.1 0.0 copy-start
  52.1 2.4 %copy.8 = f32[2,4,128,256]{3,2,1,0:T(8,128)} copy(f32[2,4,128,256]{3,2,1,0:T(8,128)} %get-tuple-element.4) | data formatting | bytes 2097152
  54.5 0.0 copy-done
  54.5 1.3 %copy.9 = f32[2,2,16,64,128]{4,3,2,1,0:T(8,128)} copy(f32[2,2,16,64,128]{4,3,2,1,0:T(8,128)S(1)} %copy-done) | data formatting | bytes 4194304
Async XLA Ops:
  52.1 2.4 %copy-start = (f32[2,2,16,64,128]{4,3,2,1,0:T(8,128)S(1)}, f32[2,2,16,64,128]{4,3,2,1,0:T(8,128)}, u32[]{:S(2)}) copy-start(f32[2,2,16,64,128]{4,3,2,1,0:T(8,128)} %get-tuple-element.5) | copy-start | bytes 6291460
where the time goes:
time: 56 us; the launch traced here: 55.8 us
  Pallas kernels  51.5 us (92%)
  local copies, waits for them, and re-layouts  3.74 us (7%)
  between operations  0.65 us (1%)
    pallas_call x1, Pallas kernels, per_device(): pl.pallas_call(functools.partial(fused_kernel, copies), in_specs=[pl.Bloc...  51.5 us
    unnamed x4, local copies, waits for them, and re-layouts  3.74 us

commit v1 on v0

--- a/solution.py
+++ b/solution.py
@@ -11,6 +11,7 @@
 MSTEPS = 4
 H = 4
 SLOT = 2 * H
+STRIP = 4 * H
 LANES = 128
 
 step_control = 0.15
@@ -219,52 +220,98 @@
     landed(got_xm)
     landed(got_mc)
 
-    mheight, mfull = rows + 2 * H, cols + LANES
+    mheight = rows + 2 * H
+    lane = lane_ids(mheight)
+    turn = lambda f, by: pltpu.roll(f, by, 1)
     up_x = lambda f: pltpu.roll(f, mheight - 1, 0)
     low_x = lambda f: pltpu.roll(f, 1, 0)
-    up_y = lambda f: pltpu.roll(f, mfull - 1, 1)
-    low_y = lambda f: pltpu.roll(f, 1, 1)
-
-    def extend(own, after, before, sides, slot):
-        own = jnp.concatenate([own, after, before], axis=0)
-        return jnp.concatenate([own, side_block(*sides, slot)], axis=1)
+
+    def up_y(f, strip, g):
+        beyond = turn(strip, (2 * LANES - 1 - (STRIP * g + 3 * H)) % LANES)
+        return jnp.where(lane == LANES - 1, beyond, turn(f, LANES - 1))
+
+    def low_y(f, strip, g):
+        return jnp.where(lane == 0, turn(strip, (LANES - (STRIP * g + H - 1)) % LANES), turn(f, 1))
+
+    def with_strip(strip, own, sides, slot, g):
+        at = lane - STRIP * g
+        from_slot = lambda to: lax.rem(to + 2 * LANES - SLOT * slot, LANES)
+        parts = (
+            turn(sides[0], from_slot(STRIP * g)),
+            turn(own, (STRIP * g + H) % LANES),
+            turn(own, (STRIP * g + 3 * H) % LANES),
+            turn(sides[1], from_slot(STRIP * g + 2 * H)),
+        )
+        for k, part in enumerate(parts):
+            strip = jnp.where((at >= k * H) & (at < (k + 1) * H), part, strip)
+        return strip
+
+    def everywhere(strip):
+        by = STRIP
+        while by < LANES:
+            strip = strip + turn(strip, by)
+            by *= 2
+        return strip
+
+    def stack_rows(own, after, before):
+        return jnp.concatenate([own, after, before], axis=0)
+
+    blank = jnp.zeros((mheight, LANES), F32)
+    odd = lax.rem(lane // STRIP, 2) == 1
 
     def weights(l):
         t = base * levels + l
-        kappa = extend(d_ref[l], nm[t], prm[t], side_values(ym_in, mcor_in, base), l)
+        kappa = stack_rows(d_ref[l], nm[t], prm[t])
+        kstrip = with_strip(blank, kappa, side_values(ym_in, mcor_in, base), l, 0)
         t = (base + 1) * levels
-        spin = extend(r_ref[...], nm[t], prm[t], side_values(ym_in, mcor_in, base + 1), 0)
-        east = (0.5 * step_member) * (kappa + up_x(kappa))
-        north = (0.5 * step_member) * (kappa + up_y(kappa))
-        return east, north, step_member * spin
-
-    def steps(p, q, east, north, spin):
-        for _ in range(MSTEPS):
+        spin = stack_rows(r_ref[...], nm[t], prm[t])
+        sstrip = with_strip(blank, spin, side_values(ym_in, mcor_in, base + 1), 0, 0)
+        half = 0.5 * step_member
+        east, north = half * (kappa + up_x(kappa)), half * (kappa + up_y(kappa, kstrip, 0))
+        kstrip = everywhere(kstrip)
+        east_s, north_s = half * (kstrip + up_x(kstrip)), half * (kstrip + turn(kstrip, LANES - 1))
+        sstrip = step_member * everywhere(sstrip)
+        return east, north, step_member * spin, east_s, north_s, jnp.where(odd, sstrip, -sstrip)
+
+    def steps(state, strip, w):
+        east, north, spin, east_s, north_s, spin_s = w
+        for step in range(MSTEPS):
+            sy = north_s * (turn(strip, LANES - 1) - strip)
             moved = []
-            for f in (p, q):
+            for g, f in enumerate(state):
                 fx = east * (up_x(f) - f)
-                fy = north * (up_y(f) - f)
-                moved.append(f + ((fx - low_x(fx)) + (fy - low_y(fy))))
-            p, q = moved[0] - spin * q, moved[1] + spin * p
-        return p[:rows, :cols], q[:rows, :cols]
+                fy = north * (up_y(f, strip, g) - f)
+                moved.append(f + ((fx - low_x(fx)) + (fy - low_y(fy, sy, g))))
+            for g in range(0, len(state), 2):
+                p, q = state[g], state[g + 1]
+                moved[g] = moved[g] - spin * q
+                moved[g + 1] = moved[g + 1] + spin * p
+            if step < MSTEPS - 1:
+                sx = east_s * (up_x(strip) - strip)
+                other = jnp.where(odd, turn(strip, STRIP), turn(strip, LANES - STRIP))
+                strip = strip + ((sx - low_x(sx)) + (sy - turn(sy, 1))) + spin_s * other
+            state = moved
+        return [f[:rows] for f in state]
 
     def member_level(l):
-        w = weights(l)
-        for m in range(count):
-            pair = []
-            for f in range(fields):
-                g = m * fields + f
-                t = g * levels + l
-                pair.append(extend(m_ref[m, f, l], nm[t], prm[t], side_values(ym_in, mcor_in, g), l))
-            mf_ref[m, 0, l], mf_ref[m, 1, l] = steps(*pair, *w)
+        state, strip = [], blank
+        for g in range(base):
+            t = g * levels + l
+            own = stack_rows(m_ref[g // fields, g % fields, l], nm[t], prm[t])
+            strip = with_strip(strip, own, side_values(ym_in, mcor_in, g), l, g)
+            state.append(own)
+        for g, f in enumerate(steps(state, strip, weights(l))):
+            mf_ref[g // fields, g % fields, l] = f
 
     def correction_level(l):
-        w = weights(me * clevels + l)
-        pair = []
+        state, strip = [], blank
         for f in range(fields):
             t = f * clevels + l
-            pair.append(extend(corr[l, f], ncorr[t], prcorr[t], side_values(ycorr_in, kcor_in, f), l))
-        shift[l, 0], shift[l, 1] = steps(*pair, *w)
+            own = stack_rows(corr[l, f], ncorr[t], prcorr[t])
+            strip = with_strip(strip, own, side_values(ycorr_in, kcor_in, f), l, f)
+            state.append(own)
+        for f, value in enumerate(steps(state, strip, weights(me * clevels + l))):
+            shift[l, f] = value
 
     cut_a, cut_b = (3 * levels) // 16, (6 * levels) // 16
     pl.loop(0, cut_a)(member_level)

time: 56 us -> 76 us (1.36)
  Pallas kernels: 51.5 us -> 71.4 us
    pallas_call x1, Pallas kernels: 51.5 us -> 71.4 us  [per_device(): pl.pallas_call(functools.partial(fused_kernel, copies), in_specs=[pl.Bloc...]
where the time goes in v1:
time: 76 us; the launch traced here: 75.8 us
  Pallas kernels  71.4 us (94%)
  local copies, waits for them, and re-layouts  3.74 us (5%)
    pallas_call x1, Pallas kernels, per_device(): pl.pallas_call(functools.partial(fused_kernel, copies), in_specs=[pl.Bloc...  71.4 us
    unnamed x4, local copies, waits for them, and re-layouts  3.74 us

profile of v1, /device:TPU:0, one launch (start us, length us, event | category | flops | bytes accessed | tf_op | source)
XLA Modules:
  0.0 75.8 jit_solution(595886978835142921)
XLA Ops:
  0.6 71.4 %fused.1 = (f32[2,4,128,256]{3,2,1,0:T(8,128)}, f32[2,2,16,64,128]{4,3,2,1,0:T(8,128)}) custom-call(f32[2,4,128,256]{3,2,1,0:T(8,128)} %c_ref.1, f32[2,2,16,64,128]{4,3,2,1,0:T(8,128)} %m_ref.1, f32[16,64,128]{2,1,0:T(8,128)} %d_ref.1, f32[64,128]{1,0:T(8,128)} %r_ref.1), custom_call_target="tpu_custom_call" | custom-call | tf_op jit(solution)/shard_map/fused/pallas_call | solution.py:368
  72.1 0.0 copy-start
  72.1 2.4 %copy.8 = f32[2,4,128,256]{3,2,1,0:T(8,128)} copy(f32[2,4,128,256]{3,2,1,0:T(8,128)} %get-tuple-element.4) | data formatting | bytes 2097152
  74.5 0.0 copy-done
  74.5 1.3 %copy.9 = f32[2,2,16,64,128]{4,3,2,1,0:T(8,128)} copy(f32[2,2,16,64,128]{4,3,2,1,0:T(8,128)S(1)} %copy-done) | data formatting | bytes 4194304
Async XLA Ops:
  72.1 2.4 %copy-start = (f32[2,2,16,64,128]{4,3,2,1,0:T(8,128)S(1)}, f32[2,2,16,64,128]{4,3,2,1,0:T(8,128)}, u32[]{:S(2)}) copy-start(f32[2,2,16,64,128]{4,3,2,1,0:T(8,128)} %get-tuple-element.5) | copy-start | bytes 6291460

commit v2 on v0

--- a/solution.py
+++ b/solution.py
@@ -12,6 +12,7 @@
 H = 4
 SLOT = 2 * H
 LANES = 128
+EIGHT = 8
 
 step_control = 0.15
 viscosity = 0.5
@@ -46,7 +47,7 @@
     copies, c_ref, m_ref, d_ref, r_ref, cf_ref, mf_ref,
     hc, tc, nc, prc, hm, tm, nm, prm, yc, ym, yc_in, ym_in, ccor, mcor, ccor_in, mcor_in,
     sums, sums_in, corr, hcorr, tcorr, ncorr, prcorr, ycorr, ycorr_in, kcor, kcor_in,
-    shift, shift_in, send_sem, recv_sem,
+    shift, shift_in, stage, rowwise, faces, send_sem, recv_sem,
 ):
     fields, clevels, crows, ccols = c_ref.shape
     count, _, levels, rows, cols = m_ref.shape
@@ -248,15 +249,93 @@
             p, q = moved[0] - spin * q, moved[1] + spin * p
         return p[:rows, :cols], q[:rows, :cols]
 
-    def member_level(l):
-        w = weights(l)
-        for m in range(count):
-            pair = []
-            for f in range(fields):
-                g = m * fields + f
+    lane = lane_ids(EIGHT)
+    pairs = range(2)
+
+    def up_pair(own, side):
+        ra, rb = pltpu.roll(own, LANES - 1, 1), pltpu.roll(side, LANES - 1, 1)
+        return jnp.where(lane == LANES - 1, rb, ra), jnp.where(lane == LANES - 1, ra, rb)
+
+    def low_pair(own, side):
+        ra, rb = pltpu.roll(own, 1, 1), pltpu.roll(side, 1, 1)
+        return jnp.where(lane == 0, rb, ra), jnp.where(lane == 0, ra, rb)
+
+    def stage_group(lg):
+        @pl.loop(0, EIGHT)
+        def _(ls):
+            l = lg * EIGHT + ls
+            at = pl.ds(pl.multiple_of(ls * mheight, EIGHT), mheight)
+
+            def put(g, value):
+                stage[g, 0, at] = value[:, :cols]
+                stage[g, 1, at] = value[:, cols:]
+
+            for g in range(base):
                 t = g * levels + l
-                pair.append(extend(m_ref[m, f, l], nm[t], prm[t], side_values(ym_in, mcor_in, g), l))
-            mf_ref[m, 0, l], mf_ref[m, 1, l] = steps(*pair, *w)
+                own = m_ref[g // fields, g % fields, l]
+                put(g, extend(own, nm[t], prm[t], side_values(ym_in, mcor_in, g), l))
+            t = base * levels + l
+            put(base, extend(d_ref[l], nm[t], prm[t], side_values(ym_in, mcor_in, base), l))
+            t = (base + 1) * levels
+            spin = extend(r_ref[...], nm[t], prm[t], side_values(ym_in, mcor_in, base + 1), 0)
+            put(base + 1, step_member * spin)
+
+        @pl.loop(0, mheight, unroll=4)
+        def _(i):
+            src = lax.rem(i + mheight - H, mheight)
+            for g in range(base + 2):
+                for b in pairs:
+                    rowwise[g, b, i] = stage[g, b, pl.ds(src, EIGHT, stride=mheight), :]
+
+        @pl.loop(0, mheight - 1, unroll=4)
+        def _(i):
+            k = [rowwise[base, b, i] for b in pairs]
+            up = up_pair(*k)
+            for b in pairs:
+                faces[0, b, i] = (0.5 * step_member) * (k[b] + rowwise[base, b, i + 1])
+                faces[1, b, i] = (0.5 * step_member) * (k[b] + up[b])
+
+    def run_group(lg):
+        for step in range(MSTEPS):
+            lo, hi = step + 1, mheight - 1 - step
+            last = step == MSTEPS - 1
+            now = [[rowwise[g, b, lo] for b in pairs] for g in range(base)]
+            flux = [
+                [faces[0, b, lo - 1] * (now[g][b] - rowwise[g, b, lo - 1]) for b in pairs]
+                for g in range(base)
+            ]
+
+            def row(i, carry):
+                now, flux = carry
+                east = [faces[0, b, i] for b in pairs]
+                north = [faces[1, b, i] for b in pairs]
+                spin = [rowwise[base + 1, b, i] for b in pairs]
+                after = [[rowwise[g, b, i + 1] for b in pairs] for g in range(base)]
+                new_flux, moved = [], []
+                for g in range(base):
+                    f = now[g]
+                    fx = [east[b] * (after[g][b] - f[b]) for b in pairs]
+                    up = up_pair(*f)
+                    fy = [north[b] * (up[b] - f[b]) for b in pairs]
+                    low = low_pair(*fy)
+                    moved.append(
+                        [f[b] + ((fx[b] - flux[g][b]) + (fy[b] - low[b])) for b in pairs]
+                    )
+                    new_flux.append(fx)
+                for g in range(0, base, 2):
+                    for b in pairs:
+                        p = moved[g][b] - spin[b] * now[g + 1][b]
+                        q = moved[g + 1][b] + spin[b] * now[g][b]
+                        if not last:
+                            rowwise[g, b, i] = p
+                            rowwise[g + 1, b, i] = q
+                        elif b == 0:
+                            for h, value in ((g, p), (g + 1, q)):
+                                at = (h * levels + lg * EIGHT) * rows + i - H
+                                mf_ref[pl.ds(at, EIGHT, stride=rows), :] = value
+                return after, new_flux
+
+            lax.fori_loop(lo, hi, row, (now, flux), unroll=2)
 
     def correction_level(l):
         w = weights(me * clevels + l)
@@ -266,16 +345,17 @@
             pair.append(extend(corr[l, f], ncorr[t], prcorr[t], side_values(ycorr_in, kcor_in, f), l))
         shift[l, 0], shift[l, 1] = steps(*pair, *w)
 
-    cut_a, cut_b = (3 * levels) // 16, (6 * levels) // 16
-    pl.loop(0, cut_a)(member_level)
+    stage_group(0)
     landed(got_yk)
     got_kc = send_corners(ycorr_in, kcor, kcor_in)
-    pl.loop(cut_a, cut_b)(member_level)
+    run_group(0)
     landed(got_xk)
     landed(got_kc)
     pl.loop(0, clevels)(correction_level)
     got_shift = [send(shift, shift_in.at[k], peers[k]) for k in range(n - 1)]
-    pl.loop(cut_b, levels)(member_level)
+    for lg in range(1, levels // EIGHT):
+        stage_group(lg)
+        run_group(lg)
 
     def add(piece, owner):
         @pl.loop(0, clevels)
@@ -283,8 +363,9 @@
             for f in range(fields):
                 tile = piece[l, f]
                 for m in range(count):
-                    at = owner * clevels + l
-                    mf_ref[m, f, at] = mf_ref[m, f, at] + tile
+                    first = ((m * fields + f) * levels + owner * clevels + l) * rows
+                    at = pl.ds(pl.multiple_of(first, EIGHT), rows)
+                    mf_ref[at, :] = mf_ref[at, :] + tile
 
     add(shift, me)
     for k in range(n - 1):
@@ -316,20 +397,23 @@
         + [vmem(fields, rows, LANES), vmem(ns, fields, rows, LANES)]
         + [vmem(ns, 2, fields, H, LANES)] * 2
         + [vmem(clevels, fields, rows, cols), vmem(n - 1, clevels, fields, rows, cols)]
+        + [vmem(base + 2, 2, EIGHT * (rows + 2 * H), LANES)]
+        + [vmem(base + 2, 2, rows + 2 * H, EIGHT, LANES), vmem(2, 2, rows + 2 * H, EIGHT, LANES)]
         + [pltpu.SemaphoreType.DMA((copies,))] * 2
     )
-    return pl.pallas_call(
+    control_final, flat = pl.pallas_call(
         functools.partial(fused_kernel, copies),
         in_specs=[pl.BlockSpec(memory_space=pltpu.VMEM)] * 4,
         out_specs=[pl.BlockSpec(memory_space=pltpu.VMEM)] * 2,
         out_shape=[
             jax.ShapeDtypeStruct(control.shape, F32),
-            jax.ShapeDtypeStruct(members.shape, F32),
+            jax.ShapeDtypeStruct((members.size // cols, cols), F32),
         ],
         scratch_shapes=scratch,
         compiler_params=pltpu.CompilerParams(collective_id=0, has_side_effects=True),
         name="fused",
     )(control, members, diffusivity, rotation)
+    return control_final, flat.reshape(members.shape)
 
 
 def solution(mesh):

time: 56 us -> 88.5 us (1.58)
  Pallas kernels: 51.5 us -> 83.9 us
    pallas_call x1, Pallas kernels: 51.5 us -> 83.9 us  [per_device(): pl.pallas_call(functools.partial(fused_kernel, copies), in_specs=[pl.Bloc...]
where the time goes in v2:
time: 88.5 us; the launch traced here: 88.3 us
  Pallas kernels  83.9 us (95%)
  local copies, waits for them, and re-layouts  3.74 us (4%)
    pallas_call x1, Pallas kernels, per_device(): pl.pallas_call(functools.partial(fused_kernel, copies), in_specs=[pl.Bloc...  83.9 us
    unnamed x4, local copies, waits for them, and re-layouts  3.74 us

profile of v2, /device:TPU:0, one launch (start us, length us, event | category | flops | bytes accessed | tf_op | source)
XLA Modules:
  0.0 88.3 jit_solution(13405568060802796304)
XLA Ops:
  0.6 83.9 %fused.1 = (f32[2,4,128,256]{3,2,1,0:T(8,128)}, f32[4096,128]{1,0:T(8,128)}) custom-call(f32[2,4,128,256]{3,2,1,0:T(8,128)} %c_ref.1, f32[2,2,16,64,128]{4,3,2,1,0:T(8,128)} %m_ref.1, f32[16,64,128]{2,1,0:T(8,128)} %d_ref.1, f32[64,128]{1,0:T(8,128)} %r_ref.1), custom_call_target="tpu_custom_call" | custom-call | tf_op jit(solution)/shard_map/fused/pallas_call | solution.py:404
  84.6 0.0 copy-start
  84.6 2.4 %copy.8 = f32[2,4,128,256]{3,2,1,0:T(8,128)} copy(f32[2,4,128,256]{3,2,1,0:T(8,128)} %get-tuple-element.8) | data formatting | bytes 2097152
  87.0 0.0 copy-done
  87.0 1.3 %copy.9 = f32[2,2,16,64,128]{4,3,2,1,0:T(8,128)} copy(f32[2,2,16,64,128]{4,3,2,1,0:T(8,128)S(1)} %bitcast.1) | data formatting | bytes 4194304
Async XLA Ops:
  84.6 2.4 %copy-start = (f32[4096,128]{1,0:T(8,128)S(1)}, f32[4096,128]{1,0:T(8,128)}, u32[]{:S(2)}) copy-start(f32[4096,128]{1,0:T(8,128)} %get-tuple-element.5) | copy-start | bytes 6291460

commit v3 on v2

--- a/solution.py
+++ b/solution.py
@@ -13,6 +13,7 @@
 SLOT = 2 * H
 LANES = 128
 EIGHT = 8
+CHUNK = 8
 
 step_control = 0.15
 viscosity = 0.5
@@ -260,6 +261,14 @@
         ra, rb = pltpu.roll(own, 1, 1), pltpu.roll(side, 1, 1)
         return jnp.where(lane == 0, rb, ra), jnp.where(lane == 0, ra, rb)
 
+    for i in (mheight, mheight + 1):
+        for b in pairs:
+            for g in range(base + 2):
+                rowwise[g, b, i] = jnp.zeros((EIGHT, LANES), F32)
+            for g in range(2):
+                faces[g, b, i] = jnp.zeros((EIGHT, LANES), F32)
+                faces[g, b, mheight - 1] = jnp.zeros((EIGHT, LANES), F32)
+
     def stage_group(lg):
         @pl.loop(0, EIGHT)
         def _(ls):
@@ -280,62 +289,79 @@
             spin = extend(r_ref[...], nm[t], prm[t], side_values(ym_in, mcor_in, base + 1), 0)
             put(base + 1, step_member * spin)
 
-        @pl.loop(0, mheight, unroll=4)
-        def _(i):
-            src = lax.rem(i + mheight - H, mheight)
+        @pl.loop(0, mheight // CHUNK)
+        def _(c):
             for g in range(base + 2):
+                values = []
+                for k in range(CHUNK):
+                    src = lax.rem(c * CHUNK + k + mheight - H, mheight)
+                    values += [stage[g, b, pl.ds(src, EIGHT, stride=mheight), :] for b in pairs]
+                for k in range(CHUNK):
+                    for b in pairs:
+                        rowwise[g, b, c * CHUNK + k] = values[2 * k + b]
+
+        @pl.loop(0, mheight // CHUNK)
+        def _(c):
+            i = c * CHUNK
+            kappa = [[rowwise[base, b, i + k] for b in pairs] for k in range(CHUNK + 1)]
+            ups = [up_pair(*kappa[k]) for k in range(CHUNK)]
+            for k in range(CHUNK):
                 for b in pairs:
-                    rowwise[g, b, i] = stage[g, b, pl.ds(src, EIGHT, stride=mheight), :]
-
-        @pl.loop(0, mheight - 1, unroll=4)
-        def _(i):
-            k = [rowwise[base, b, i] for b in pairs]
-            up = up_pair(*k)
+                    faces[0, b, i + k] = (0.5 * step_member) * (kappa[k][b] + kappa[k + 1][b])
+                    faces[1, b, i + k] = (0.5 * step_member) * (kappa[k][b] + ups[k][b])
+
+    def run_group(lg):
+        for g in range(0, base, 2):
+            for step in range(MSTEPS):
+                run_pair(lg, g, step == MSTEPS - 1)
+
+    def run_pair(lg, g, last):
+        lo = H if last else 1
+        chunks = (rows if last else mheight) // CHUNK
+        tiles = [(h, b) for h in (g, g + 1) for b in pairs]
+        now = [rowwise[h, b, lo] for h, b in tiles]
+        flux = [faces[0, b, lo - 1] * (rowwise[h, b, lo] - rowwise[h, b, lo - 1]) for h, b in tiles]
+
+        def chunk(c, carry):
+            now, flux = carry
+            i = lo + c * CHUNK
+            ks = range(CHUNK)
+            f = [[now[t]] + [rowwise[h, b, i + 1 + k] for k in ks] for t, (h, b) in enumerate(tiles)]
+            east = [[faces[0, b, i + k] for k in ks] for b in pairs]
+            north = [[faces[1, b, i + k] for k in ks] for b in pairs]
+            spin = [[rowwise[base + 1, b, i + k] for k in ks] for b in pairs]
+            fx = [
+                [flux[t]] + [east[b][k] * (f[t][k + 1] - f[t][k]) for k in ks]
+                for t, (h, b) in enumerate(tiles)
+            ]
+            out = []
+            for first in (0, 2):
+                up = [up_pair(f[first][k], f[first + 1][k]) for k in ks]
+                fy = [[north[b][k] * (up[k][b] - f[first + b][k]) for k in ks] for b in pairs]
+                low = [low_pair(fy[0][k], fy[1][k]) for k in ks]
+                for b in pairs:
+                    t = first + b
+                    out.append(
+                        [
+                            f[t][k] + ((fx[t][k + 1] - fx[t][k]) + (fy[b][k] - low[k][b]))
+                            for k in ks
+                        ]
+                    )
             for b in pairs:
-                faces[0, b, i] = (0.5 * step_member) * (k[b] + rowwise[base, b, i + 1])
-                faces[1, b, i] = (0.5 * step_member) * (k[b] + up[b])
-
-    def run_group(lg):
-        for step in range(MSTEPS):
-            lo, hi = step + 1, mheight - 1 - step
-            last = step == MSTEPS - 1
-            now = [[rowwise[g, b, lo] for b in pairs] for g in range(base)]
-            flux = [
-                [faces[0, b, lo - 1] * (now[g][b] - rowwise[g, b, lo - 1]) for b in pairs]
-                for g in range(base)
-            ]
-
-            def row(i, carry):
-                now, flux = carry
-                east = [faces[0, b, i] for b in pairs]
-                north = [faces[1, b, i] for b in pairs]
-                spin = [rowwise[base + 1, b, i] for b in pairs]
-                after = [[rowwise[g, b, i + 1] for b in pairs] for g in range(base)]
-                new_flux, moved = [], []
-                for g in range(base):
-                    f = now[g]
-                    fx = [east[b] * (after[g][b] - f[b]) for b in pairs]
-                    up = up_pair(*f)
-                    fy = [north[b] * (up[b] - f[b]) for b in pairs]
-                    low = low_pair(*fy)
-                    moved.append(
-                        [f[b] + ((fx[b] - flux[g][b]) + (fy[b] - low[b])) for b in pairs]
-                    )
-                    new_flux.append(fx)
-                for g in range(0, base, 2):
-                    for b in pairs:
-                        p = moved[g][b] - spin[b] * now[g + 1][b]
-                        q = moved[g + 1][b] + spin[b] * now[g][b]
-                        if not last:
-                            rowwise[g, b, i] = p
-                            rowwise[g + 1, b, i] = q
-                        elif b == 0:
-                            for h, value in ((g, p), (g + 1, q)):
-                                at = (h * levels + lg * EIGHT) * rows + i - H
-                                mf_ref[pl.ds(at, EIGHT, stride=rows), :] = value
-                return after, new_flux
-
-            lax.fori_loop(lo, hi, row, (now, flux), unroll=2)
+                if last and b == 1:
+                    continue
+                for k in ks:
+                    p = out[b][k] - spin[b][k] * f[2 + b][k]
+                    q = out[2 + b][k] + spin[b][k] * f[b][k]
+                    for h, value in ((g, p), (g + 1, q)):
+                        if last:
+                            at = (h * levels + lg * EIGHT) * rows + c * CHUNK + k
+                            mf_ref[pl.ds(at, EIGHT, stride=rows), :] = value
+                        else:
+                            rowwise[h, b, i + k] = value
+            return [f[t][CHUNK] for t in range(4)], [fx[t][CHUNK] for t in range(4)]
+
+        lax.fori_loop(0, chunks, chunk, (now, flux))
 
     def correction_level(l):
         w = weights(me * clevels + l)
@@ -398,7 +424,7 @@
         + [vmem(ns, 2, fields, H, LANES)] * 2
         + [vmem(clevels, fields, rows, cols), vmem(n - 1, clevels, fields, rows, cols)]
         + [vmem(base + 2, 2, EIGHT * (rows + 2 * H), LANES)]
-        + [vmem(base + 2, 2, rows + 2 * H, EIGHT, LANES), vmem(2, 2, rows + 2 * H, EIGHT, LANES)]
+        + [vmem(base + 2, 2, rows + 2 * H + 2, EIGHT, LANES), vmem(2, 2, rows + 2 * H + 2, EIGHT, LANES)]
         + [pltpu.SemaphoreType.DMA((copies,))] * 2
     )
     control_final, flat = pl.pallas_call(

time: 88.5 us -> 69.9 us (0.79)
  Pallas kernels: 83.9 us -> 65.4 us
    pallas_call x1, Pallas kernels: 83.9 us -> 65.4 us  [per_device(): pl.pallas_call(functools.partial(fused_kernel, copies), in_specs=[pl.Bloc...]
where the time goes in v3:
time: 69.9 us; the launch traced here: 69.8 us
  Pallas kernels  65.4 us (94%)
  local copies, waits for them, and re-layouts  3.74 us (5%)
    pallas_call x1, Pallas kernels, per_device(): pl.pallas_call(functools.partial(fused_kernel, copies), in_specs=[pl.Bloc...  65.4 us
    unnamed x4, local copies, waits for them, and re-layouts  3.74 us

profile of v3, /device:TPU:0, one launch (start us, length us, event | category | flops | bytes accessed | tf_op | source)
XLA Modules:
  0.0 69.8 jit_solution(17564892112261276246)
XLA Ops:
  0.6 65.4 %fused.1 = (f32[2,4,128,256]{3,2,1,0:T(8,128)}, f32[4096,128]{1,0:T(8,128)}) custom-call(f32[2,4,128,256]{3,2,1,0:T(8,128)} %c_ref.1, f32[2,2,16,64,128]{4,3,2,1,0:T(8,128)} %m_ref.1, f32[16,64,128]{2,1,0:T(8,128)} %d_ref.1, f32[64,128]{1,0:T(8,128)} %r_ref.1), custom_call_target="tpu_custom_call" | custom-call | tf_op jit(solution)/shard_map/fused/pallas_call | solution.py:430
  66.0 0.0 copy-start
  66.0 2.4 %copy.8 = f32[2,4,128,256]{3,2,1,0:T(8,128)} copy(f32[2,4,128,256]{3,2,1,0:T(8,128)} %get-tuple-element.8) | data formatting | bytes 2097152
  68.5 0.0 copy-done
  68.5 1.3 %copy.9 = f32[2,2,16,64,128]{4,3,2,1,0:T(8,128)} copy(f32[2,2,16,64,128]{4,3,2,1,0:T(8,128)S(1)} %bitcast.1) | data formatting | bytes 4194304
Async XLA Ops:
  66.0 2.4 %copy-start = (f32[4096,128]{1,0:T(8,128)S(1)}, f32[4096,128]{1,0:T(8,128)}, u32[]{:S(2)}) copy-start(f32[4096,128]{1,0:T(8,128)} %get-tuple-element.5) | copy-start | bytes 6291460

commit v4 on v0

--- a/solution.py
+++ b/solution.py
@@ -197,9 +197,10 @@
             t = jnp.dot(pick_x, t, precision=lax.Precision.HIGHEST, preferred_element_type=F32)
             corr[l, f] = 0.25 * t
 
+    pl.loop(0, 1)(control_level)
     landed(got_ym)
     got_mc = send_corners(ym_in, mcor, mcor_in)
-    pl.loop(0, clevels)(control_level)
+    pl.loop(1, clevels)(control_level)
     landed(got_sum)
 
     @pl.loop(0, clevels)

time: 56 us -> 55.9 us (level)
  no operation moved by 1% of the time
where the time goes in v4:
time: 55.9 us; the launch traced here: 55.7 us
  Pallas kernels  51.3 us (92%)
  local copies, waits for them, and re-layouts  3.74 us (7%)
  between operations  0.65 us (1%)
    pallas_call x1, Pallas kernels, per_device(): pl.pallas_call(functools.partial(fused_kernel, copies), in_specs=[pl.Bloc...  51.3 us
    unnamed x4, local copies, waits for them, and re-layouts  3.74 us

profile of v4, /device:TPU:0, one launch (start us, length us, event | category | flops | bytes accessed | tf_op | source)
XLA Modules:
  0.0 55.7 jit_solution(8377943868476852755)
XLA Ops:
  0.6 51.3 %fused.1 = (f32[2,4,128,256]{3,2,1,0:T(8,128)}, f32[2,2,16,64,128]{4,3,2,1,0:T(8,128)}) custom-call(f32[2,4,128,256]{3,2,1,0:T(8,128)} %c_ref.1, f32[2,2,16,64,128]{4,3,2,1,0:T(8,128)} %m_ref.1, f32[16,64,128]{2,1,0:T(8,128)} %d_ref.1, f32[64,128]{1,0:T(8,128)} %r_ref.1), custom_call_target="tpu_custom_call" | custom-call | tf_op jit(solution)/shard_map/fused/pallas_call | solution.py:322
  52.0 0.0 copy-start
  52.0 2.4 %copy.8 = f32[2,4,128,256]{3,2,1,0:T(8,128)} copy(f32[2,4,128,256]{3,2,1,0:T(8,128)} %get-tuple-element.4) | data formatting | bytes 2097152
  54.4 0.0 copy-done
  54.4 1.3 %copy.9 = f32[2,2,16,64,128]{4,3,2,1,0:T(8,128)} copy(f32[2,2,16,64,128]{4,3,2,1,0:T(8,128)S(1)} %copy-done) | data formatting | bytes 4194304
Async XLA Ops:
  52.0 2.4 %copy-start = (f32[2,2,16,64,128]{4,3,2,1,0:T(8,128)S(1)}, f32[2,2,16,64,128]{4,3,2,1,0:T(8,128)}, u32[]{:S(2)}) copy-start(f32[2,2,16,64,128]{4,3,2,1,0:T(8,128)} %get-tuple-element.5) | copy-start | bytes 6291460
